TPU v7x, 256 devices: a whole 4x4x8 slice. The times are simulated.
256 devices in a mesh: lat: 32 (over x_lo, z, core), ch: 8 (over y, x_hi).
Axes of the slice: x: 4 (x_hi: 2, x_lo: 2; x = x_hi * 2 + x_lo), y: 4, z: 8, core: 2. Of those that a mesh axis runs over, the one named last changes fastest.
Arguments:
- spectrum: bfloat16 [512, 64, 2, 2, 256], P('lat', 'ch'), may hold values from -0.01953125 to 0.01953125
- legendre: bfloat16 [640, 256, 512], P('lat'), as said below
- block_slots: int32 [32], replicated, may hold values from 0 to 31, each once
- kernel_values: bfloat16 [3, 640, 6, 9], P(None, 'lat'), may hold values from -2 to 2
- near_rows: int32 [640, 6], P('lat'), may hold values from 0 to 639, as said below
- mix_weights: bfloat16 [3, 64, 64], replicated, may hold values from -0.4375 to 0.4375
Outputs:
- convolved: bfloat16 [64, 640, 1440], P('ch', 'lat')
Inputs may be any that keep to these rules, and one draw needn't show every extreme that they name: legendre[r, k, m] is zero where m + 2 * k + p >= 512, with p = 0 for r < 320 and p = 1 otherwise. near_rows[r, q] lies within 2 rows of r; slot 0 holds max(r - 2, 0) and slot 1 holds min(r + 2, 639). `block_slots`: each order block appears once.
All inputs are finite; a program needn't handle non-finite values.
Results may differ from a plain program's by a relative error of at most 0.005.
Values may be sent and summed in bfloat16 or wider, within the bound.
No kernel may reach another device: no remote copies, remote signals or barrier semaphores. Data moves between devices by JAX's collectives and lax.ppermute only.
A program may use at most 320 MiB of HBM per device.

v0:
```python
import math
import jax
import jax.numpy as jnp
from jax import lax
from jax.sharding import PartitionSpec as P

NLON = 1440
LMAX = 512
ORDER_BLOCK = 16
KER = 3
REACH = 2
LON_REACH = 4
TAPS = 9


def padded_2(shard, sides, width):
    for axis, dim in sides:
        count, length = (lax.axis_size(axis), shard.shape[dim])
        up = [(i, (i + 1) % count) for i in range(count - 1)]
        down = [(j, i) for i, j in up]
        last = lax.slice_in_dim(shard, length - width, length, axis=dim)
        first = lax.slice_in_dim(shard, 0, width, axis=dim)
        before = lax.ppermute(last, axis, up)
        after = lax.ppermute(first, axis, down)
        shard = jnp.concatenate([before, shard, after], axis=dim)
    return shard


def fourier_table():
    orders = jnp.arange(LMAX, dtype=jnp.int32)
    places = jnp.arange(NLON, dtype=jnp.int32)
    phases = orders[:, None] * places[None, :] % NLON
    angles = phases.astype(jnp.float32) * (2.0 * math.pi / NLON)
    weight = jnp.where(orders == 0, 1.0, 2.0).astype(jnp.float32)[:, None]
    return jnp.concatenate([weight * jnp.cos(angles), -weight * jnp.sin(angles)], axis=0)


def per_device(spectrum, legendre, block_slots, kernel_values, near_rows, mix_weights):
    lat_count = lax.axis_size("lat")
    lat_index = lax.axis_index("lat")
    ch_index = lax.axis_index("ch")
    row_count = legendre.shape[0]
    chan_dev = spectrum.shape[1]
    northern = lat_index < lat_count // 2
    parity = jnp.where(northern, 0, 1).astype(jnp.int32)
    zero_sum = jnp.zeros((row_count, chan_dev, 2, LMAX), jnp.float32)
    chosen = lax.dynamic_index_in_dim(
        lax.all_gather(spectrum, "lat", axis=0, tiled=True), parity, 2, keepdims=False
    )
    slot_rows = jnp.arange(chosen.shape[0], dtype=jnp.int32)
    order_ids = block_slots[slot_rows // ORDER_BLOCK] * ORDER_BLOCK + slot_rows % ORDER_BLOCK
    columns = jnp.take(legendre, order_ids, axis=2)
    contribution = jnp.einsum("rkn,ncxk->rcxn", columns, chosen, preferred_element_type=jnp.float32)
    partial_sum = zero_sum.at[:, :, :, order_ids].add(contribution)
    split_sums = partial_sum.reshape(row_count, chan_dev, 2, lat_count, LMAX // lat_count)
    by_source = lax.all_to_all(split_sums, "lat", split_axis=3, concat_axis=3, tiled=True)
    flipped = by_source[:, :, :, ::-1]
    returned = lax.all_to_all(flipped, "lat", split_axis=3, concat_axis=3, tiled=True)
    mirrored = returned.reshape(row_count, chan_dev, 2, LMAX)
    mirror_sign = jnp.where(northern, -1.0, 1.0).astype(jnp.float32)
    spectral = partial_sum + mirror_sign * mirrored[::-1]
    grid_field = jnp.dot(
        spectral.reshape(row_count * chan_dev, 2 * LMAX),
        fourier_table(),
        precision=lax.Precision.HIGHEST,
        preferred_element_type=jnp.float32,
    )
    grid_field = grid_field.reshape(row_count, chan_dev, NLON).astype(jnp.bfloat16)
    local_rows = near_rows - (lat_index * row_count - REACH)
    padded = padded_2(grid_field, (("lat", 0),), REACH)
    gathered = jnp.take(padded, local_rows, axis=0)
    spread = jnp.zeros((KER, row_count, chan_dev, NLON), jnp.float32)
    for offset in range(TAPS):
        rolled = jnp.roll(gathered, LON_REACH - offset, axis=3)
        spread = spread + jnp.einsum(
            "kiq,iqcx->kicx",
            kernel_values[:, :, :, offset],
            rolled,
            preferred_element_type=jnp.float32,
        )
    own_weights = lax.dynamic_slice_in_dim(mix_weights, ch_index * chan_dev, chan_dev, 1)
    weight_cols = own_weights.astype(jnp.float32)
    return lax.psum_scatter(
        jnp.einsum("kcd,kicx->dix", weight_cols, spread, precision=lax.Precision.HIGHEST),
        "ch",
        scatter_dimension=0,
        tiled=True,
    ).astype(jnp.bfloat16)


def solution(mesh):
    return jax.shard_map(
        per_device,
        mesh=mesh,
        in_specs=(
            P("lat", "ch", None, None, None),
            P("lat", None, None),
            P(),
            P(None, "lat", None, None),
            P("lat", None),
            P(),
        ),
        out_specs=P("ch", "lat", None),
        check_vma=False,
    )
```

profile of v0, /device:TPU:1, one launch (start us, length us, event | category | flops | bytes accessed | tf_op | source)
XLA Modules:
  0.0 490.7 jit_solution(12187650134679098284)
XLA Ops:
  6.5 1.7 copy.19
  8.3 8.9 %copy.18 = bf16[20,256,512]{1,0,2:T(8,128)(2,1)} copy(bf16[20,256,512]{2,1,0:T(8,128)(2,1)} %param.7) | data formatting | bytes 10485760 | tf_op args[1]
  18.1 0.7 fusion.90
  18.8 4.5 compare_select_fusion.3
  23.3 0.7 fusion.89
  24.0 16.1 %compare_and_fusion.1 = (pred[512]{0:T(512)(128)(4,1)S(1)}, s32[512]{0:T(512)S(1)}) fusion(pred[512]{0:T(512)(128)(4,1)S(1)} %compare_reduce_fusion, pred[512]{0:T(512)(128)(4,1)S(1)} %compare_reduce_fusion.1, pred[512]{0:T(512)(128)(4,1)S(1)} %compare_reduce_fusion.2, pred[512]{0:T(512)(128)(4,1)S(1)} %compare_reduce_fusion.3, ...), kind=kLoop, calls=%fused_computation.126 | loop fusion | flops 19968 | bytes 17508 | tf_op jit(solution)/shard_map/jit(_take)/and | solution.py:52
  40.2 6.4 %gather_fusion = bf16[512,20,256]{2,1,0:T(8,128)(2,1)} fusion(bf16[20,256,512]{1,0,2:T(8,128)(2,1)} %copy.18, s32[1024]{0:T(1024)S(1)} %pad_clamp_fusion.1), kind=kCustom, calls=%fused_computation | custom fusion | bytes 10487808 | tf_op jit(solution)/shard_map/jit(_take)/gather | solution.py:52
  46.6 39.5 %all-gather.2.cloned.1.call-done = bf16[512,8,2,2,256]{4,1,3,2,0:T(8,128)(2,1)} async-done(((bf16[16,8,2,2,256]{4,1,3,2,0:T(8,128)(2,1)}), bf16[512,8,2,2,256]{4,1,3,2,0:T(8,128)(2,1)}) %all-gather.2.cloned.1.call-update) | async-done | bytes 8388624 | tf_op jit(solution)/shard_map/all_gather | solution.py:48
  86.1 7.8 %fusion = f32[512,20,8,2]{1,2,3,0:T(8,128)} fusion(bf16[512,20,256]{2,1,0:T(8,128)(2,1)} %gather_fusion, pred[512]{0:T(512)(128)(4,1)S(1)} %get-tuple-element.7, bf16[512,8,2,2,256]{4,1,3,2,0:T(8,128)(2,1)} %all-gather.2.cloned.1.call-done, s32[]{:T(128)S(6)} %select_n.109), kind=kOutput, calls=%fused_computation.3 | convolution fusion | flops 86507520 | bytes 11141636 | tf_op jit(solution)/shard_map/rkn,ncxk->rcxn/dot_general | solution.py:53
  93.9 2.2 broadcast_in_dim.39
  96.1 61.8 %scatter_fusion = f32[20,8,2,512]{0,1,3,2:T(8,128)} fusion(f32[20,8,2,512]{0,1,3,2:T(8,128)} %broadcast_in_dim.39, s32[512]{0:T(512)S(1)} %bitcast.115, f32[512,20,8,2]{1,2,3,0:T(8,128)} %fusion), kind=kCustom, calls=%fused_computation.2 | custom fusion | flops 163840 | bytes 1968128 | tf_op jit(solution)/shard_map/scatter-add | solution.py:54
  157.9 4.7 copy.60
  162.5 6.5 %reshape.292 = f32[32,1,5120]{2,1,0:T(1,128)} reshape(f32[32,2,16,8,20]{4,3,2,1,0:T(8,128)} %bitcast.113) | data formatting | bytes 1310720
  169.0 6.6 %all-to-all-start = ((f32[32,1,5120]{2,1,0:T(1,128)}), f32[32,1,5120]{2,1,0:T(1,128)S(1)}, u32[]{:S(2)}, u32[]{:S(2)}) async-start(f32[32,1,5120]{2,1,0:T(1,128)} %reshape.292), calls=%async_computation | async-start | bytes 1310720 | tf_op jit(solution)/shard_map/all_to_all | solution.py:56
  175.6 18.8 %all-to-all-done = f32[32,1,5120]{2,1,0:T(1,128)S(1)} async-done(((f32[32,1,5120]{2,1,0:T(1,128)}), f32[32,1,5120]{2,1,0:T(1,128)S(1)}, u32[]{:S(2)}, u32[]{:S(2)}) %all-to-all-start) | async-done | bytes 655392 | tf_op jit(solution)/shard_map/all_to_all | solution.py:56
  194.4 0.5 broadcast.497
  194.9 2.2 reduce.50
  197.1 6.2 %reshape.293 = f32[32,2,16,8,20]{4,3,2,1,0:T(8,128)} reshape(f32[32,5120]{1,0:T(8,128)S(1)} %reduce.50) | data formatting | bytes 1310720
  203.3 4.7 reverse_bitcast_fusion
  208.0 6.5 %reshape.294 = f32[32,1,5120]{2,1,0:T(1,128)} reshape(f32[32,2,16,8,20]{4,3,2,1,0:T(8,128)} %reverse_bitcast_fusion) | data formatting | bytes 1310720
  214.5 6.4 %all-to-all-start.1 = ((f32[32,1,5120]{2,1,0:T(1,128)}), f32[32,1,5120]{2,1,0:T(1,128)}, u32[]{:S(2)}, u32[]{:S(2)}) async-start(f32[32,1,5120]{2,1,0:T(1,128)} %reshape.294), calls=%async_computation.1 | async-start | bytes 1310720 | tf_op jit(solution)/shard_map/all_to_all | solution.py:58
  220.9 0.2 reduce-scatter.2.cloned.1.call-start
  221.2 0.6 reshape.161
  221.8 0.6 fusion.88
  222.4 13.3 %sine_multiply_fusion = (f32[512,1440]{0,1:T(8,128)S(1)}, f32[512,1440]{0,1:T(8,128)}) fusion(f32[512]{0:T(512)S(1)} %fusion.66, f32[512]{0:T(512)S(1)} %fusion.65), kind=kLoop, calls=%fused_computation.54 | loop fusion | flops 8110080 | bytes 5902336 | tf_op jit(solution)/shard_map/mul | solution.py:35
  235.7 4.3 all-to-all-done.1
  240.0 4.2 reduce.51
  244.2 7.2 %reshape.295 = f32[32,2,16,8,20]{4,3,2,1,0:T(8,128)} reshape(f32[32,5120]{1,0:T(8,128)} %reduce.51) | data formatting | bytes 1310720
  251.4 4.7 copy.21
  256.1 7.3 %rev.7 = f32[20,8,2,512]{0,1,3,2:T(8,128)} reverse(f32[20,8,2,512]{0,1,3,2:T(8,128)} %bitcast.112), dimensions={0} | reverse | bytes 1310720 | tf_op jit(solution)/shard_map/rev | solution.py:61
  263.3 5.8 %multiply_add_fusion = f32[20,8,2,512]{0,1,3,2:T(8,128)} fusion(f32[20,8,2,512]{0,1,3,2:T(8,128)} %scatter_fusion, f32[20,8,2,512]{0,1,3,2:T(8,128)} %rev.7, f32[]{:T(128)S(6)} %select_n.113), kind=kLoop, calls=%fused_computation.14 | loop fusion | flops 327680 | bytes 1966084 | tf_op jit(solution)/shard_map/add | solution.py:61
  269.2 3.8 copy.22
  273.0 7.5 %fusion.48 = bf16[20,8,1440]{2,1,0:T(8,128)(2,1)S(1)} fusion(f32[20,8,1024]{2,1,0:T(8,128)} %copy.22, f32[512,1440]{0,1:T(8,128)S(1)} %get-tuple-element.68, f32[512,1440]{0,1:T(8,128)} %get-tuple-element.69), kind=kOutput, calls=%fused_computation.60 | convolution fusion | flops 2832860160 | bytes 7014400 | tf_op jit(solution)/shard_map/dot_general | solution.py:62
  280.5 5.1 %collective-permute-start = (bf16[2,8,1440]{2,1,0:T(8,128)(2,1)S(1)}, bf16[2,8,1440]{2,1,0:T(8,128)(2,1)S(1)}, u32[]{:S(2)}, u32[]{:S(2)}) collective-permute-start(bf16[2,8,1440]{2,1,0:T(8,128)(2,1)S(1)} %get-tuple-element.25), channel_id=1, source_target_pairs={{0,8},{8,16},{16,24},{24,32},{32,40},{40,48},{48,56},{56,64},{64,7... | collective-permute-start | bytes 138248 | tf_op jit(solution)/shard_map/ppermute | solution.py:23
  285.6 2.1 collective-permute-start.1
  287.8 0.7 copy.17
  288.5 0.7 copy.50
  289.2 0.8 copy.53
  290.0 1.4 copy.52
  291.4 0.7 copy.51
  292.1 0.7 copy.49
  292.9 0.7 copy.48
  293.6 0.7 copy.47
  294.4 0.8 copy.54
  295.3 0.9 pad_maximum_fusion
  296.2 1.9 gather_fusion.1
  298.1 1.1 copy_select_fusion
  299.6 0.2 fusion.79
  300.0 4.2 fusion.86
  304.2 4.2 fusion.84
  308.4 2.3 fusion.80
  310.7 2.5 fusion.82
  313.3 3.6 fusion.21
  316.9 5.2 %fusion.25 = f32[20,8,1440,3]{2,3,1,0:T(4,128)} fusion(bf16[20,6,8,1]{3,1,2,0:T(8,128)(2,1)S(1)} %get-tuple-element.22, bf16[20,6,8,1439]{3,1,2,0:T(8,128)(2,1)} %get-tuple-element.24, bf16[3,20,6,1]{2,0,1,3:T(4,128)(2,1)S(1)} %copy-done.4), kind=kOutput, calls=%fused_computation.32 | convolution fusion | flops 13824000 | bytes 5530320 | tf_op jit(solution)/shard_map/kiq,iqcx->kicx/dot_general | solution.py:75
  322.1 5.5 %fusion.17 = f32[20,8,1440,3]{2,3,1,0:T(4,128)} fusion(bf16[20,6,8,1438]{3,1,2,0:T(8,128)(2,1)} %get-tuple-element.19, bf16[20,6,8,2]{3,1,2,0:T(8,128)(2,1)S(1)} %get-tuple-element.17, bf16[3,20,6,1]{2,0,1,3:T(4,128)(2,1)S(1)} %copy-done.5), kind=kOutput, calls=%fused_computation.24 | convolution fusion | flops 13824000 | bytes 5530320 | tf_op jit(solution)/shard_map/kiq,iqcx->kicx/dot_general | solution.py:75
  327.6 5.3 %fusion.29 = f32[20,8,1440,3]{2,3,1,0:T(4,128)} fusion(bf16[20,6,8,2]{3,1,2,0:T(8,128)(2,1)S(1)} %get-tuple-element.18, bf16[20,6,8,1438]{3,1,2,0:T(8,128)(2,1)} %get-tuple-element.20, bf16[3,20,6,1]{2,0,1,3:T(4,128)(2,1)S(1)} %copy-done.2), kind=kOutput, calls=%fused_computation.36 | convolution fusion | flops 13824000 | bytes 5530320 | tf_op jit(solution)/shard_map/kiq,iqcx->kicx/dot_general | solution.py:75
  332.9 3.4 fusion.13
  336.3 3.2 fusion.33
  339.5 3.3 fusion.9
  342.8 3.2 fusion.37
  346.0 13.6 %add_bitcast_fusion = f32[3,20,8,1440]{3,0,2,1:T(4,128)} fusion(f32[20,8,1440,3]{2,3,1,0:T(4,128)} %fusion.37, f32[20,8,1440,3]{2,3,1,0:T(4,128)} %fusion.33, f32[20,8,1440,3]{2,3,1,0:T(4,128)} %fusion.29, f32[20,8,1440,3]{2,3,1,0:T(4,128)} %fusion.25, f32[20,8,1440,3]{2,3,1,0:T(4,128)S(1)} %fusion.21, f32[20,8,1440,3]{2,3,1,0:T(4,128)} %fusion.17, ...), kind=kOutput, calls=%fused_computation.49 | convolution fusion | flops 15206400 | bytes 27648840 | tf_op jit(solution)/shard_map/kiq,iqcx->kicx/dot_general | solution.py:75
  359.6 8.7 %convolution_bitcast_fusion = f32[64,20,1440]{2,0,1:T(8,128)} fusion(f32[3,20,8,1440]{3,0,2,1:T(4,128)} %add_bitcast_fusion, bf16[3,64,64]{2,1,0:T(8,128)(2,1)S(1)} %copy-done, s32[]{:T(128)S(6)} %select_n.103), kind=kOutput, calls=%fused_computation.11 | convolution fusion | flops 530841600 | bytes 10143748 | tf_op jit(solution)/shard_map/kcd,kicx->dix/dot_general | solution.py:84
  368.3 113.0 %reduce-scatter.2.cloned.1.call-done = f32[8,20,1440]{2,0,1:T(8,128)} async-done(((f32[64,20,1440]{2,0,1:T(8,128)}), f32[8,20,1440]{2,0,1:T(8,128)}) %reduce-scatter.2.cloned.1.call-update) | async-done | bytes 921616 | tf_op jit(solution)/shard_map/reduce_scatter | solution.py:83
  481.4 2.0 convert_element_type.14
  (66 shorter events, 1.8 us)
Async XLA Ops:
  6.5 353.1 %copy-start = (bf16[3,64,64]{2,1,0:T(8,128)(2,1)S(1)}, bf16[3,64,64]{2,1,0:T(8,128)(2,1)}, u32[]{:S(2)}) copy-start(bf16[3,64,64]{2,1,0:T(8,128)(2,1)} %param.11) | copy-start | bytes 73732
  6.5 79.5 %all-gather.2.cloned.1.call-start = ((), (), s32[]{:S(2)}) async-start(), calls=%async_computation.3 | async-start | bytes 8650752 | tf_op jit(solution)/shard_map/all_gather | solution.py:48
  8.3 9.8 %copy-start.1 = (s32[32]{0:T(128)S(1)}, s32[32]{0:T(128)}, u32[]{:S(2)}) copy-start(s32[32]{0:T(128)} %param.8) | copy-start | bytes 388
  169.0 25.4 %all-to-all-start = ((f32[32,1,5120]{2,1,0:T(1,128)}), f32[32,1,5120]{2,1,0:T(1,128)S(1)}, u32[]{:S(2)}, u32[]{:S(2)}) async-start(f32[32,1,5120]{2,1,0:T(1,128)} %reshape.292), calls=%async_computation | async-start | bytes 1310720 | tf_op jit(solution)/shard_map/all_to_all | solution.py:56
  208.0 13.1 %copy-start.10 = (s32[20,6]{0,1:T(8,128)S(1)}, s32[20,6]{0,1:T(8,128)}, u32[]{:S(2)}) copy-start(s32[20,6]{0,1:T(8,128)} %param.10) | copy-start | bytes 1444
  208.0 13.8 %copy-start.8 = (bf16[3,20,6,9]{1,2,3,0:T(8,128)(2,1)S(1)}, bf16[3,20,6,9]{1,2,3,0:T(8,128)(2,1)}, u32[]{:S(2)}) copy-start(bf16[3,20,6,9]{1,2,3,0:T(8,128)(2,1)} %param.9) | copy-start | bytes 19444
  214.5 25.6 %all-to-all-start.1 = ((f32[32,1,5120]{2,1,0:T(1,128)}), f32[32,1,5120]{2,1,0:T(1,128)}, u32[]{:S(2)}, u32[]{:S(2)}) async-start(f32[32,1,5120]{2,1,0:T(1,128)} %reshape.294), calls=%async_computation.1 | async-start | bytes 1310720 | tf_op jit(solution)/shard_map/all_to_all | solution.py:58
  220.9 260.5 %reduce-scatter.2.cloned.1.call-start = ((), (), s32[]{:S(2)}) async-start(), calls=%async_computation.4 | async-start | bytes 8847360 | tf_op jit(solution)/shard_map/reduce_scatter | solution.py:83
  273.0 14.8 %copy-start.11 = (s32[120]{0:T(128)S(1)}, s32[120]{0:T(128)}, u32[]{:S(2)}) copy-start(s32[120]{0:T(128)} %reshape.161) | copy-start | bytes 1444
  280.5 14.8 %collective-permute-start = (bf16[2,8,1440]{2,1,0:T(8,128)(2,1)S(1)}, bf16[2,8,1440]{2,1,0:T(8,128)(2,1)S(1)}, u32[]{:S(2)}, u32[]{:S(2)}) collective-permute-start(bf16[2,8,1440]{2,1,0:T(8,128)(2,1)S(1)} %get-tuple-element.25), channel_id=1, source_target_pairs={{0,8},{8,16},{16,24},{24,32},{32,40},{40,48},{48,56},{56,64},{64,7... | collective-permute-start | bytes 138248 | tf_op jit(solution)/shard_map/ppermute | solution.py:23
  285.6 9.7 %collective-permute-start.1 = (bf16[2,8,1440]{2,1,0:T(8,128)(2,1)S(1)}, bf16[2,8,1440]{2,1,0:T(8,128)(2,1)S(1)}, u32[]{:S(2)}, u32[]{:S(2)}) collective-permute-start(bf16[2,8,1440]{2,1,0:T(8,128)(2,1)S(1)} %get-tuple-element.26), channel_id=1, source_target_pairs={{8,0},{16,8},{24,16},{32,24},{40,32},{48,40},{56,48},{64,56},{72,6... | collective-permute-start | bytes 138248 | tf_op jit(solution)/shard_map/ppermute | solution.py:24
  296.2 1.9 copy-start.9
  310.7 2.6 copy-start.6
  313.3 3.6 copy-start.4
  316.9 5.2 %copy-start.5 = (bf16[3,20,6,1]{2,0,1,3:T(4,128)(2,1)S(1)}, bf16[3,20,6,1]{2,0,1,3:T(4,128)(2,1)}, u32[]{:S(2)}) copy-start(bf16[3,20,6,1]{2,0,1,3:T(4,128)(2,1)} %copy.48) | copy-start | bytes 2164
  322.1 5.5 %copy-start.2 = (bf16[3,20,6,1]{2,0,1,3:T(4,128)(2,1)S(1)}, bf16[3,20,6,1]{2,0,1,3:T(4,128)(2,1)}, u32[]{:S(2)}) copy-start(bf16[3,20,6,1]{2,0,1,3:T(4,128)(2,1)} %copy.52) | copy-start | bytes 2164
  327.6 5.3 %copy-start.3 = (bf16[3,20,6,1]{2,0,1,3:T(4,128)(2,1)S(1)}, bf16[3,20,6,1]{2,0,1,3:T(4,128)(2,1)}, u32[]{:S(2)}) copy-start(bf16[3,20,6,1]{2,0,1,3:T(4,128)(2,1)} %copy.47) | copy-start | bytes 2164
  342.8 3.2 copy-start.7
Sparse Core Ops, SparseCore 0:
  9.2 76.7 all-gather.1
  368.5 112.8 reduce-scatter.1
where the time goes:
time: 499 us; the launch traced here: 491 us
  waiting for transfers between devices  176 us (35%)
  other arithmetic  113 us (23%)
  local copies, waits for them, and re-layouts  97.3 us (19%)
  matrix products  70.3 us (14%)
  starting transfers between devices  20.4 us (4%)
  between operations  14.2 us (3%)
    reduce_scatter x1, waiting for transfers between devices, per_device(): lax.psum_scatter(jnp.einsum('kcd,kicx->dix', weight_cols, spread, precisi...  113 us
    scatter-add x1, other arithmetic, per_device(): partial_sum = zero_sum.at[:, :, :, order_ids].add(contribution)  61.8 us
    unnamed x40, local copies, waits for them, and re-layouts  48.5 us
    dot_general x9, matrix products, per_device(): jnp.einsum('kiq,iqcx->kicx', kernel_values[:, :, :, offset], rolled, pref...  46.3 us
    all_gather x1, waiting for transfers between devices, per_device(): lax.all_gather(spectrum, 'lat', axis=0, tiled=True)  39.5 us
    all_to_all x1, waiting for transfers between devices, per_device(): lax.all_to_all(split_sums, 'lat', split_axis=3, concat_axis=3, tiled=True)  18.8 us
    and x1, other arithmetic, per_device(): columns = jnp.take(legendre, order_ids, axis=2)  16.1 us
    slice x8, local copies, waits for them, and re-layouts, per_device(): rolled = jnp.roll(gathered, LON_REACH - offset, axis=3)  14 us
  transfers between devices with their start and end apart: 6, of which 4 were waited for; matrix products, arithmetic and copies ran while one was open for 12% of the time, Pallas kernels for 0%

commit v1 on v0

--- a/solution.py
+++ b/solution.py
@@ -45,7 +45,12 @@
     parity = jnp.where(northern, 0, 1).astype(jnp.int32)
     zero_sum = jnp.zeros((row_count, chan_dev, 2, LMAX), jnp.float32)
     chosen = lax.dynamic_index_in_dim(
-        lax.all_gather(spectrum, "lat", axis=0, tiled=True), parity, 2, keepdims=False
+        jnp.concatenate(
+            lax.all_to_all(jnp.stack([spectrum] * lax.axis_size("lat")), "lat", 0, 0), axis=0
+        ),
+        parity,
+        2,
+        keepdims=False,
     )
     slot_rows = jnp.arange(chosen.shape[0], dtype=jnp.int32)
     order_ids = block_slots[slot_rows // ORDER_BLOCK] * ORDER_BLOCK + slot_rows % ORDER_BLOCK

time: 499 us -> 630 us (1.26)
  waiting for transfers between devices: 176 us -> 283 us
  starting transfers between devices: 20.4 us -> 35.8 us
  local copies, waits for them, and re-layouts: 97.3 us -> 108 us
    all_to_all x0 -> x1, waiting for transfers between devices: none -> 147 us  [per_device(): lax.all_to_all(jnp.stack([spectrum] * lax.axis_size('lat')), 'lat', 0, 0)]
    all_gather x1 -> x0, waiting for transfers between devices: 39.5 us -> none  [per_device(): lax.all_gather(spectrum, 'lat', axis=0, tiled=True)]
    all_to_all x0 -> x1, starting transfers between devices: none -> 11.1 us  [per_device(): lax.all_to_all(jnp.stack([spectrum] * lax.axis_size('lat')), 'lat', 0, 0)]
    all_to_all x0 -> x1, local copies, waits for them, and re-layouts: none -> 7.83 us  [per_device(): lax.all_to_all(jnp.stack([spectrum] * lax.axis_size('lat')), 'lat', 0, 0)]
    unnamed x40 -> x42, local copies, waits for them, and re-layouts: 48.5 us -> 47.6 us
  transfers between devices with their start and end apart: 6 -> 6, of which waited for: 4 -> 4; matrix products, arithmetic and copies ran while one was open for 12% -> 10% of each run, Pallas kernels for 0% -> 0%
where the time goes in v1:
time: 630 us; the launch traced here: 622 us
  waiting for transfers between devices  283 us (45%)
  other arithmetic  112 us (18%)
  local copies, waits for them, and re-layouts  108 us (17%)
  matrix products  67.6 us (11%)
  starting transfers between devices  35.8 us (6%)
  between operations  14.2 us (2%)
    all_to_all x1, waiting for transfers between devices, per_device(): lax.all_to_all(jnp.stack([spectrum] * lax.axis_size('lat')), 'lat', 0, 0)  147 us
    reduce_scatter x1, waiting for transfers between devices, per_device(): lax.psum_scatter(jnp.einsum('kcd,kicx->dix', weight_cols, spread, precisi...  114 us
    scatter-add x1, other arithmetic, per_device(): partial_sum = zero_sum.at[:, :, :, order_ids].add(contribution)  61.8 us
    unnamed x42, local copies, waits for them, and re-layouts  47.6 us
    dot_general x9, matrix products, per_device(): jnp.einsum('kiq,iqcx->kicx', kernel_values[:, :, :, offset], rolled, pref...  46.3 us
    all_to_all x1, waiting for transfers between devices, per_device(): lax.all_to_all(split_sums, 'lat', split_axis=3, concat_axis=3, tiled=True)  18.8 us
    and x1, other arithmetic, per_device(): columns = jnp.take(legendre, order_ids, axis=2)  15.6 us
    slice x8, local copies, waits for them, and re-layouts, per_device(): rolled = jnp.roll(gathered, LON_REACH - offset, axis=3)  14 us
  transfers between devices with their start and end apart: 6, of which 4 were waited for; matrix products, arithmetic and copies ran while one was open for 10% of the time, Pallas kernels for 0%

profile of v1, /device:TPU:1, one launch (start us, length us, event | category | flops | bytes accessed | tf_op | source)
XLA Modules:
  0.0 621.5 jit_solution(7775017970923469442)
XLA Ops:
  6.5 1.0 copy.37
  7.5 4.2 stack.2
  11.8 11.1 %all-to-all-start = ((bf16[32,16,8,2,2,256]{5,2,4,1,3,0:T(8,128)(2,1)}), bf16[32,16,8,2,2,256]{5,2,4,1,3,0:T(8,128)(2,1)}, u32[]{:S(2)}, u32[]{:S(2)}) async-start(bf16[32,16,8,2,2,256]{5,2,4,1,3,0:T(8,128)(2,1)} %stack.2), calls=%async_computation | async-start | bytes 16777216 | tf_op jit(solution)/shard_map/all_to_all | solution.py:49
  22.9 8.9 %copy.36 = bf16[20,256,512]{1,0,2:T(8,128)(2,1)} copy(bf16[20,256,512]{2,1,0:T(8,128)(2,1)} %param.7) | data formatting | bytes 10485760 | tf_op args[1]
  32.6 0.7 fusion.90
  33.3 4.3 compare_select_fusion.3
  37.6 0.7 fusion.89
  38.3 15.6 %compare_and_fusion.1 = (pred[512]{0:T(512)(128)(4,1)S(1)}, s32[512]{0:T(512)S(1)}) fusion(pred[512]{0:T(512)(128)(4,1)S(1)} %compare_reduce_fusion, pred[512]{0:T(512)(128)(4,1)S(1)} %compare_reduce_fusion.1, pred[512]{0:T(512)(128)(4,1)S(1)} %compare_reduce_fusion.2, pred[512]{0:T(512)(128)(4,1)S(1)} %compare_reduce_fusion.3, ...), kind=kLoop, calls=%fused_computation.126 | loop fusion | flops 19968 | bytes 17508 | tf_op jit(solution)/shard_map/jit(_take)/and | solution.py:57
  53.9 6.4 %gather_fusion = bf16[512,20,256]{2,1,0:T(8,128)(2,1)} fusion(bf16[20,256,512]{1,0,2:T(8,128)(2,1)} %copy.36, s32[1024]{0:T(1024)S(1)} %pad_clamp_fusion.1), kind=kCustom, calls=%fused_computation | custom fusion | bytes 10487808 | tf_op jit(solution)/shard_map/jit(_take)/gather | solution.py:57
  60.4 146.6 %all-to-all-done = bf16[32,16,8,2,2,256]{5,2,4,1,3,0:T(8,128)(2,1)} async-done(((bf16[32,16,8,2,2,256]{5,2,4,1,3,0:T(8,128)(2,1)}), bf16[32,16,8,2,2,256]{5,2,4,1,3,0:T(8,128)(2,1)}, u32[]{:S(2)}, u32[]{:S(2)}) %all-to-all-start) | async-done | bytes 8388640 | tf_op jit(solution)/shard_map/all_to_all | solution.py:49
  206.9 7.8 %copy.38 = bf16[32,16,8,2,2,256]{5,2,4,3,1,0:T(8,128)(2,1)} copy(bf16[32,16,8,2,2,256]{5,2,4,1,3,0:T(8,128)(2,1)} %all-to-all-done) | data formatting | bytes 16777216 | tf_op jit(solution)/shard_map/all_to_all | solution.py:49
  214.8 5.1 fusion
  219.9 2.2 broadcast_in_dim.39
  222.1 61.8 %scatter_fusion = f32[20,8,2,512]{0,1,3,2:T(8,128)} fusion(f32[20,8,2,512]{0,1,3,2:T(8,128)} %broadcast_in_dim.39, s32[512]{0:T(512)S(1)} %bitcast.117, f32[512,20,8,2]{1,2,3,0:T(8,128)} %fusion), kind=kCustom, calls=%fused_computation.2 | custom fusion | flops 163840 | bytes 1968128 | tf_op jit(solution)/shard_map/scatter-add | solution.py:59
  283.9 4.6 copy.79
  288.5 6.5 %reshape.298 = f32[32,1,5120]{2,1,0:T(1,128)} reshape(f32[32,2,16,8,20]{4,3,2,1,0:T(8,128)} %bitcast.114) | data formatting | bytes 1310720
  294.9 10.9 %all-to-all-start.1 = ((f32[32,1,5120]{2,1,0:T(1,128)}), f32[32,1,5120]{2,1,0:T(1,128)S(1)}, u32[]{:S(2)}, u32[]{:S(2)}) async-start(f32[32,1,5120]{2,1,0:T(1,128)} %reshape.298), calls=%async_computation.1 | async-start | bytes 1310720 | tf_op jit(solution)/shard_map/all_to_all | solution.py:61
  305.9 18.8 %all-to-all-done.1 = f32[32,1,5120]{2,1,0:T(1,128)S(1)} async-done(((f32[32,1,5120]{2,1,0:T(1,128)}), f32[32,1,5120]{2,1,0:T(1,128)S(1)}, u32[]{:S(2)}, u32[]{:S(2)}) %all-to-all-start.1) | async-done | bytes 655392 | tf_op jit(solution)/shard_map/all_to_all | solution.py:61
  325.2 2.2 reduce.50
  327.4 6.2 reshape.299
  333.6 4.6 reverse_bitcast_fusion
  338.2 6.5 %reshape.300 = f32[32,1,5120]{2,1,0:T(1,128)} reshape(f32[32,2,16,8,20]{4,3,2,1,0:T(8,128)} %reverse_bitcast_fusion) | data formatting | bytes 1310720
  344.7 6.4 %all-to-all-start.2 = ((f32[32,1,5120]{2,1,0:T(1,128)}), f32[32,1,5120]{2,1,0:T(1,128)}, u32[]{:S(2)}, u32[]{:S(2)}) async-start(f32[32,1,5120]{2,1,0:T(1,128)} %reshape.300), calls=%async_computation.2 | async-start | bytes 1310720 | tf_op jit(solution)/shard_map/all_to_all | solution.py:63
  351.4 0.6 reshape.167
  352.0 0.6 fusion.88
  352.6 13.3 %sine_multiply_fusion = (f32[512,1440]{0,1:T(8,128)S(1)}, f32[512,1440]{0,1:T(8,128)}) fusion(f32[512]{0:T(512)S(1)} %fusion.66, f32[512]{0:T(512)S(1)} %fusion.65), kind=kLoop, calls=%fused_computation.54 | loop fusion | flops 8110080 | bytes 5902336 | tf_op jit(solution)/shard_map/mul | solution.py:35
  365.9 4.3 all-to-all-done.2
  370.2 4.2 reduce.51
  374.4 7.1 %reshape.301 = f32[32,2,16,8,20]{4,3,2,1,0:T(8,128)} reshape(f32[32,5120]{1,0:T(8,128)} %reduce.51) | data formatting | bytes 1310720
  381.6 4.7 copy.40
  386.2 7.2 %rev.7 = f32[20,8,2,512]{0,1,3,2:T(8,128)} reverse(f32[20,8,2,512]{0,1,3,2:T(8,128)} %bitcast.113), dimensions={0} | reverse | bytes 1310720 | tf_op jit(solution)/shard_map/rev | solution.py:66
  393.5 5.8 multiply_add_fusion
  399.3 3.8 copy.41
  403.1 7.5 %fusion.48 = bf16[20,8,1440]{2,1,0:T(8,128)(2,1)S(1)} fusion(f32[20,8,1024]{2,1,0:T(8,128)} %copy.41, f32[512,1440]{0,1:T(8,128)S(1)} %get-tuple-element.68, f32[512,1440]{0,1:T(8,128)} %get-tuple-element.69), kind=kOutput, calls=%fused_computation.60 | convolution fusion | flops 2832860160 | bytes 7014400 | tf_op jit(solution)/shard_map/dot_general | solution.py:67
  410.6 5.1 collective-permute-start
  415.7 2.1 collective-permute-start.1
  417.9 0.7 copy.35
  418.5 0.7 copy.69
  419.3 0.8 copy.72
  420.1 1.4 copy.71
  421.5 0.7 copy.70
  422.2 0.7 copy.68
  422.9 0.7 copy.67
  423.7 0.7 copy.66
  424.5 0.8 copy.73
  425.4 0.9 pad_maximum_fusion
  426.2 1.9 gather_fusion.1
  428.1 1.1 copy_select_fusion
  430.1 4.2 fusion.86
  434.3 4.2 fusion.84
  438.5 2.3 fusion.80
  440.8 2.5 fusion.82
  443.4 3.6 fusion.21
  447.0 5.2 fusion.25
  452.2 5.5 fusion.17
  457.7 5.3 fusion.29
  463.0 3.4 fusion.13
  466.4 3.2 fusion.33
  469.5 3.3 fusion.9
  472.9 3.2 fusion.37
  476.0 13.6 %add_bitcast_fusion = f32[3,20,8,1440]{3,0,2,1:T(4,128)} fusion(f32[20,8,1440,3]{2,3,1,0:T(4,128)} %fusion.37, f32[20,8,1440,3]{2,3,1,0:T(4,128)} %fusion.33, f32[20,8,1440,3]{2,3,1,0:T(4,128)} %fusion.29, f32[20,8,1440,3]{2,3,1,0:T(4,128)} %fusion.25, f32[20,8,1440,3]{2,3,1,0:T(4,128)S(1)} %fusion.21, f32[20,8,1440,3]{2,3,1,0:T(4,128)} %fusion.17, ...), kind=kOutput, calls=%fused_computation.49 | convolution fusion | flops 15206400 | bytes 27648840 | tf_op jit(solution)/shard_map/kiq,iqcx->kicx/dot_general | solution.py:80
  489.7 8.7 %convolution_bitcast_fusion = f32[64,20,1440]{2,0,1:T(8,128)} fusion(f32[3,20,8,1440]{3,0,2,1:T(4,128)} %add_bitcast_fusion, bf16[3,64,64]{2,1,0:T(8,128)(2,1)S(1)} %copy-done, s32[]{:T(128)S(6)} %select_n.103), kind=kOutput, calls=%fused_computation.11 | convolution fusion | flops 530841600 | bytes 10143748 | tf_op jit(solution)/shard_map/kcd,kicx->dix/dot_general | solution.py:89
  498.4 113.7 %reduce-scatter.2.cloned.1.call-done = f32[8,20,1440]{2,0,1:T(8,128)} async-done(((f32[64,20,1440]{2,0,1:T(8,128)}), f32[8,20,1440]{2,0,1:T(8,128)}) %reduce-scatter.2.cloned.1.call-update) | async-done | bytes 921616 | tf_op jit(solution)/shard_map/reduce_scatter | solution.py:88
  612.1 2.0 convert_element_type.14
  (69 shorter events, 2.7 us)
Async XLA Ops:
  6.5 483.1 %copy-start = (bf16[3,64,64]{2,1,0:T(8,128)(2,1)S(1)}, bf16[3,64,64]{2,1,0:T(8,128)(2,1)}, u32[]{:S(2)}) copy-start(bf16[3,64,64]{2,1,0:T(8,128)(2,1)} %param.11) | copy-start | bytes 73732
  11.8 195.2 %all-to-all-start = ((bf16[32,16,8,2,2,256]{5,2,4,1,3,0:T(8,128)(2,1)}), bf16[32,16,8,2,2,256]{5,2,4,1,3,0:T(8,128)(2,1)}, u32[]{:S(2)}, u32[]{:S(2)}) async-start(bf16[32,16,8,2,2,256]{5,2,4,1,3,0:T(8,128)(2,1)} %stack.2), calls=%async_computation | async-start | bytes 16777216 | tf_op jit(solution)/shard_map/all_to_all | solution.py:49
  22.9 9.8 %copy-start.2 = (s32[32]{0:T(128)S(1)}, s32[32]{0:T(128)}, u32[]{:S(2)}) copy-start(s32[32]{0:T(128)} %param.8) | copy-start | bytes 388
  206.9 7.8 %copy-start.1 = (bf16[512,20,256]{2,1,0:T(8,128)(2,1)S(1)}, bf16[512,20,256]{2,1,0:T(8,128)(2,1)}, u32[]{:S(2)}) copy-start(bf16[512,20,256]{2,1,0:T(8,128)(2,1)} %gather_fusion) | copy-start | bytes 15728644
  294.9 29.7 %all-to-all-start.1 = ((f32[32,1,5120]{2,1,0:T(1,128)}), f32[32,1,5120]{2,1,0:T(1,128)S(1)}, u32[]{:S(2)}, u32[]{:S(2)}) async-start(f32[32,1,5120]{2,1,0:T(1,128)} %reshape.298), calls=%async_computation.1 | async-start | bytes 1310720 | tf_op jit(solution)/shard_map/all_to_all | solution.py:61
  338.2 13.1 %copy-start.11 = (s32[20,6]{0,1:T(8,128)S(1)}, s32[20,6]{0,1:T(8,128)}, u32[]{:S(2)}) copy-start(s32[20,6]{0,1:T(8,128)} %param.10) | copy-start | bytes 1444
  338.2 13.8 %copy-start.9 = (bf16[3,20,6,9]{1,2,3,0:T(8,128)(2,1)S(1)}, bf16[3,20,6,9]{1,2,3,0:T(8,128)(2,1)}, u32[]{:S(2)}) copy-start(bf16[3,20,6,9]{1,2,3,0:T(8,128)(2,1)} %param.9) | copy-start | bytes 19444
  344.7 25.6 %all-to-all-start.2 = ((f32[32,1,5120]{2,1,0:T(1,128)}), f32[32,1,5120]{2,1,0:T(1,128)}, u32[]{:S(2)}, u32[]{:S(2)}) async-start(f32[32,1,5120]{2,1,0:T(1,128)} %reshape.300), calls=%async_computation.2 | async-start | bytes 1310720 | tf_op jit(solution)/shard_map/all_to_all | solution.py:63
  351.0 261.1 %reduce-scatter.2.cloned.1.call-start = ((), (), s32[]{:S(2)}) async-start(), calls=%async_computation.4 | async-start | bytes 8847360 | tf_op jit(solution)/shard_map/reduce_scatter | solution.py:88
  403.1 14.8 %copy-start.12 = (s32[120]{0:T(128)S(1)}, s32[120]{0:T(128)}, u32[]{:S(2)}) copy-start(s32[120]{0:T(128)} %reshape.167) | copy-start | bytes 1444
  410.6 14.8 %collective-permute-start = (bf16[2,8,1440]{2,1,0:T(8,128)(2,1)S(1)}, bf16[2,8,1440]{2,1,0:T(8,128)(2,1)S(1)}, u32[]{:S(2)}, u32[]{:S(2)}) collective-permute-start(bf16[2,8,1440]{2,1,0:T(8,128)(2,1)S(1)} %get-tuple-element.25), channel_id=1, source_target_pairs={{0,8},{8,16},{16,24},{24,32},{32,40},{40,48},{48,56},{56,64},{64,7... | collective-permute-start | bytes 138248 | tf_op jit(solution)/shard_map/ppermute | solution.py:23
  415.7 9.7 %collective-permute-start.1 = (bf16[2,8,1440]{2,1,0:T(8,128)(2,1)S(1)}, bf16[2,8,1440]{2,1,0:T(8,128)(2,1)S(1)}, u32[]{:S(2)}, u32[]{:S(2)}) collective-permute-start(bf16[2,8,1440]{2,1,0:T(8,128)(2,1)S(1)} %get-tuple-element.26), channel_id=1, source_target_pairs={{8,0},{16,8},{24,16},{32,24},{40,32},{48,40},{56,48},{64,56},{72,6... | collective-permute-start | bytes 138248 | tf_op jit(solution)/shard_map/ppermute | solution.py:24
  426.2 1.9 copy-start.10
  440.8 2.6 copy-start.7
  443.3 3.6 copy-start.5
  446.9 5.2 copy-start.6
  452.2 5.5 copy-start.3
  457.7 5.3 copy-start.4
  472.9 3.2 copy-start.8
Sparse Core Ops, SparseCore 0:
  498.5 113.5 reduce-scatter.1
